TPU v7x, 512 devices: a whole 4x4x16 slice. The times are simulated.
512 devices in a mesh: ep: 16 (over z), mx: 4 (over x), my: 8 (over y, core).
Axes of the slice: x: 4, y: 4, z: 16, core: 2. Of those that a mesh axis runs over, the one named last changes fastest.
Arguments:
- context: bfloat16 [16384, 2048], P(('ep', 'mx')), may hold values from -6 to 6
- resid_in: bfloat16 [16384, 2048], P(('ep', 'mx'), 'my'), may hold values from -70 to 70
- out_weight: bfloat16 [2048, 2048], P(None, 'my'), may hold values from -0.125 to 0.125
- norm_gain: float32 [2048], P('my'), may hold values from 0.5 to 1.5
- gate_weight: bfloat16 [8, 5632, 2048], P(None, ('ep', 'my'), 'mx'), may hold values from -0.125 to 0.125
- up_weight: bfloat16 [8, 5632, 2048], P(None, ('ep', 'my'), 'mx'), may hold values from -0.125 to 0.125
- down_weight: bfloat16 [8, 5632, 2048], P(None, ('ep', 'my'), 'mx'), may hold values from -0.078125 to 0.078125
- routes: int32 [16384, 2], P(('ep', 'mx')), may hold values from 0 to 7, all different within a row; in each aligned block of 256 rows (0 to 255, 256 to 511, ...) at most 96 rows name the same one
- gate_probs: float32 [16384, 2], P(('ep', 'mx')), may hold values from 0.05 to 1
- final_gain: float32 [2048], P('my'), may hold values from 0.5 to 1.5
Outputs:
- normed_out: bfloat16 [16384, 2048], P(('ep', 'mx'), 'my')
- stream_out: bfloat16 [16384, 2048], P(('ep', 'mx'), 'my')
Inputs may be any that keep to these rules, and one draw needn't show every extreme that they name: `routes`: each row names 2 different experts; in each aligned block of 256 rows no expert is named by more than 96 rows, a bound that some block reaches.
All inputs are finite; a program needn't handle non-finite values.
Results may differ from a plain program's by a relative error of at most 0.012.
Values may be sent and summed in bfloat16 or wider, within the bound.
A program may use at most 128 MiB of HBM per device.

v0:
```python
import jax
import jax.numpy as jnp
import numpy as np
from jax import lax
from jax.sharding import PartitionSpec as P

D = 2048
EXPERTS = 8
TOPK = 2
MOST = 96
EPSILON = 1e-06


def row_scale(stream_f):
    partial_sq = jnp.sum(stream_f * stream_f, axis=1)
    row_total = lax.psum(partial_sq, "my")
    return lax.rsqrt(row_total / D + EPSILON)


def shards(
    context,
    resid_in,
    out_weight,
    norm_gain,
    gate_weight,
    up_weight,
    down_weight,
    routes,
    gate_probs,
    final_gain,
):
    ep_count = lax.axis_size("ep")
    mx_count = lax.axis_size("mx")
    slot_dev = max(1, EXPERTS // ep_count)
    slot_total = slot_dev * ep_count
    replicas = slot_total // EXPERTS
    capacity = MOST // replicas
    tok_rows = context.shape[0]
    feat_block = resid_in.shape[1]
    piece_units = gate_weight.shape[1]
    width_block = gate_weight.shape[2]
    slot_rows = ep_count * capacity
    projected = jnp.dot(context, out_weight, preferred_element_type=jnp.float32)
    stream = (projected + resid_in.astype(jnp.float32)).astype(jnp.bfloat16)
    stream_f = stream.astype(jnp.float32)
    normed = (stream_f * row_scale(stream_f)[:, None] * norm_gain[None, :]).astype(jnp.bfloat16)
    chosen = routes.reshape(-1)
    onehot = (chosen[:, None] == jnp.arange(EXPERTS, dtype=jnp.int32)[None, :]).astype(jnp.int32)
    before = jnp.cumsum(onehot, axis=0) - onehot
    ranking = jnp.sum(before * onehot, axis=1)
    slot_index = chosen * replicas + ranking % replicas
    target = slot_index * capacity + ranking // replicas
    row_ids = jnp.arange(tok_rows * TOPK, dtype=jnp.int32) // TOPK
    source = jnp.full((slot_total * capacity,), tok_rows, jnp.int32).at[target].set(row_ids)
    padded = jnp.concatenate([normed, jnp.zeros((1, feat_block), jnp.bfloat16)], axis=0)
    packed = padded[source].reshape(ep_count, slot_dev, capacity, feat_block)
    landed = lax.all_to_all(packed, "ep", split_axis=0, concat_axis=0, tiled=True)
    gathered = lax.all_gather(landed, "my", axis=3, tiled=True)
    tokens_in = jnp.transpose(gathered, (1, 0, 2, 3)).reshape(slot_dev, slot_rows, D)
    split_rows = tokens_in.reshape(slot_dev, slot_rows, mx_count, width_block)
    expert_table = (
        np.arange(ep_count)[:, None] * slot_dev + np.arange(slot_dev)[None, :]
    ) // replicas

    def widen_pieces(weight):
        chosen_rows = weight[expert_table]
        wide = jnp.broadcast_to(
            chosen_rows[:, None], (ep_count, mx_count, slot_dev, piece_units, width_block)
        )
        return wide.reshape(ep_count * mx_count, slot_dev, piece_units, width_block)

    got_gate, got_up, got_down = (
        lax.all_to_all(
            widen_pieces(gate_weight), ("ep", "mx"), split_axis=0, concat_axis=0, tiled=True
        ),
        lax.all_to_all(
            widen_pieces(up_weight), ("ep", "mx"), split_axis=0, concat_axis=0, tiled=True
        ),
        lax.all_to_all(
            widen_pieces(down_weight), ("ep", "mx"), split_axis=0, concat_axis=0, tiled=True
        ),
    )
    dims_five = (ep_count, mx_count, slot_dev, piece_units, width_block)
    gate_proj = jnp.einsum(
        "jrad,sajfd->jrsf",
        split_rows,
        got_gate.reshape(dims_five),
        preferred_element_type=jnp.float32,
    )
    up_proj = jnp.einsum(
        "jrad,sajfd->jrsf",
        split_rows,
        got_up.reshape(dims_five),
        preferred_element_type=jnp.float32,
    )
    hidden = (jax.nn.silu(gate_proj) * up_proj).astype(jnp.bfloat16)
    expert_out = jnp.einsum(
        "jrsf,sajfd->jrad", hidden, got_down.reshape(dims_five), preferred_element_type=jnp.float32
    )
    expert_out = expert_out.reshape(slot_dev, slot_rows, D)
    summed = lax.psum_scatter(
        expert_out.astype(jnp.bfloat16), "my", scatter_dimension=2, tiled=True
    )
    sent_back = summed.reshape(slot_dev, ep_count, capacity, feat_block)
    sent_back = jnp.transpose(sent_back, (1, 0, 2, 3))
    returned = lax.all_to_all(sent_back, "ep", split_axis=0, concat_axis=0, tiled=True).reshape(
        slot_total * capacity, feat_block
    )
    picked = returned[target].reshape(tok_rows, TOPK, feat_block).astype(jnp.float32)
    weights_norm = gate_probs / jnp.sum(gate_probs, axis=1, keepdims=True)
    mixed = jnp.sum(weights_norm[:, :, None] * picked, axis=1)
    updated = stream_f + mixed
    normed_out = (updated * row_scale(updated)[:, None] * final_gain[None, :]).astype(jnp.bfloat16)
    return (normed_out, updated.astype(jnp.bfloat16))


def solution(mesh):
    placed = (
        P(("ep", "mx"), None),
        P(("ep", "mx"), "my"),
        P(None, "my"),
        P("my"),
        P(None, ("ep", "my"), "mx"),
        P(None, ("ep", "my"), "mx"),
        P(None, ("ep", "my"), "mx"),
        P(("ep", "mx"), None),
        P(("ep", "mx"), None),
        P("my"),
    )
    return jax.shard_map(
        shards,
        mesh=mesh,
        in_specs=placed,
        out_specs=(P(("ep", "mx"), "my"), P(("ep", "mx"), "my")),
        check_vma=False,
    )
```

profile of v0, /device:TPU:4, one launch (start us, length us, event | category | flops | bytes accessed | tf_op | source)
XLA Modules:
  0.0 643.5 jit_solution(12226968780941671538)
XLA Ops:
  7.2 0.9 copy.30
  9.1 1.1 reduce-window.6
  10.9 2.4 scatter_custom_fusion
  13.4 1.8 multiply_reduce_fusion.2
  15.2 14.9 %psum.14 = f32[256]{0:T(256)S(1)} all-reduce(f32[256]{0:T(256)S(1)} %get-tuple-element.4), channel_id=1, replica_groups=mesh['ep'=16,'mx'=4,'my'=8] {'my'}, use_global_device_ids=true, to_apply=%region_2.0 | all-reduce | flops 256 | bytes 2048 | tf_op jit(solution)/shard_map/psum | solution.py:16
  30.2 3.3 gather_fusion
  33.5 15.2 %all-to-all-start = ((bf16[16,1,48,256]{3,2,1,0:T(8,128)(2,1)}), bf16[16,1,48,256]{3,2,1,0:T(8,128)(2,1)}, u32[]{:S(2)}, u32[]{:S(2)}) async-start(bf16[16,1,48,256]{3,2,1,0:T(8,128)(2,1)} %bitcast.5), calls=%async_computation | async-start | bytes 786432 | tf_op jit(solution)/shard_map/all_to_all | solution.py:57
  48.8 2.6 gather_fusion.1
  51.8 18.0 %all-to-all-done = bf16[16,1,48,256]{3,2,1,0:T(8,128)(2,1)} async-done(((bf16[16,1,48,256]{3,2,1,0:T(8,128)(2,1)}), bf16[16,1,48,256]{3,2,1,0:T(8,128)(2,1)}, u32[]{:S(2)}, u32[]{:S(2)}) %all-to-all-start) | async-done | bytes 393248 | tf_op jit(solution)/shard_map/all_to_all | solution.py:57
  69.8 2.1 broadcast_in_dim.59
  71.9 10.2 %all-to-all-start.1 = ((bf16[64,1,44,512]{3,2,1,0:T(8,128)(2,1)}), bf16[64,1,44,512]{3,2,1,0:T(8,128)(2,1)}, u32[]{:S(2)}, u32[]{:S(2)}) async-start(bf16[64,1,44,512]{3,2,1,0:T(8,128)(2,1)} %bitcast.87), calls=%async_computation.1 | async-start | bytes 6291456 | tf_op jit(solution)/shard_map/all_to_all | solution.py:73
  82.2 2.6 gather_fusion.3
  85.2 140.9 %all-to-all-done.1 = bf16[64,1,44,512]{3,2,1,0:T(8,128)(2,1)} async-done(((bf16[64,1,44,512]{3,2,1,0:T(8,128)(2,1)}), bf16[64,1,44,512]{3,2,1,0:T(8,128)(2,1)}, u32[]{:S(2)}, u32[]{:S(2)}) %all-to-all-start.1) | async-done | bytes 2883616 | tf_op jit(solution)/shard_map/all_to_all | solution.py:73
  226.1 2.1 broadcast_in_dim.67
  228.2 6.3 all-to-all-start.3
  234.5 2.6 gather_fusion.2
  237.6 140.7 %all-to-all-done.3 = bf16[64,1,44,512]{3,2,1,0:T(8,128)(2,1)} async-done(((bf16[64,1,44,512]{3,2,1,0:T(8,128)(2,1)}), bf16[64,1,44,512]{3,2,1,0:T(8,128)(2,1)}, u32[]{:S(2)}, u32[]{:S(2)}) %all-to-all-start.3) | async-done | bytes 2883616 | tf_op jit(solution)/shard_map/all_to_all | solution.py:79
  378.3 2.1 broadcast_in_dim.63
  380.4 6.1 all-to-all-start.2
  387.3 43.5 %all-gather.2.cloned.1.call-done = bf16[16,1,48,2048]{3,2,1,0:T(8,128)(2,1)} async-done(((bf16[16,1,48,256]{3,2,1,0:T(8,128)(2,1)}), bf16[16,1,48,2048]{3,2,1,0:T(8,128)(2,1)}) %all-gather.2.cloned.1.call-update) | async-done | bytes 3145744 | tf_op jit(solution)/shard_map/all_gather | solution.py:58
  430.8 6.2 reshape.196
  436.9 5.7 copy.61
  442.6 6.7 %dot_general.20 = bf16[2048,44,16]{0,2,1:T(8,128)(2,1)} reshape(bf16[4,512,44,16]{1,0,3,2:T(4,128)(2,1)} %bitcast.88) | data formatting | bytes 5767168 | tf_op jit(solution)/shard_map/jrsf,sajfd->jrad/dot_general | solution.py:97
  449.3 6.9 %fusion.2 = f32[768,16,44,1]{0,2,3,1:T(8,128)} fusion(bf16[768,4,512]{2,1,0:T(4,128)(2,1)} %reshape.196, bf16[16,4,44,512]{3,2,1,0:T(8,128)(2,1)} %bitcast.80), kind=kOutput, calls=%fused_computation.9 | convolution fusion | flops 2214592512 | bytes 8192000 | tf_op jit(solution)/shard_map/jrad,sajfd->jrsf/dot_general | solution.py:84
  456.2 73.2 %all-to-all-done.2 = bf16[64,1,44,512]{3,2,1,0:T(8,128)(2,1)} async-done(((bf16[64,1,44,512]{3,2,1,0:T(8,128)(2,1)}), bf16[64,1,44,512]{3,2,1,0:T(8,128)(2,1)}, u32[]{:S(2)}, u32[]{:S(2)}) %all-to-all-start.2) | async-done | bytes 2883616 | tf_op jit(solution)/shard_map/all_to_all | solution.py:76
  529.4 16.1 %fusion.7 = bf16[1,768,2048]{2,1,0:T(8,128)(2,1)} fusion(bf16[2048,44,16]{0,2,1:T(8,128)(2,1)} %dot_general.20, f32[768,16,44,1]{0,2,3,1:T(8,128)} %fusion.2, bf16[768,4,512]{2,1,0:T(4,128)(2,1)} %reshape.196, bf16[16,4,44,512]{3,2,1,0:T(8,128)(2,1)} %bitcast.83), kind=kOutput, calls=%fused_computation.14 | convolution fusion | flops 4434001920 | bytes 14221312 | tf_op jit(solution)/shard_map/jrsf,sajfd->jrad/dot_general | solution.py:97
  545.6 37.8 %reduce-scatter.2.cloned.1.call-done = bf16[1,768,256]{2,1,0:T(8,128)(2,1)} async-done(((bf16[1,768,2048]{2,1,0:T(8,128)(2,1)}), bf16[1,768,256]{2,1,0:T(8,128)(2,1)}) %reduce-scatter.2.cloned.1.call-update) | async-done | bytes 393232 | tf_op jit(solution)/shard_map/reduce_scatter | solution.py:101
  583.4 12.4 %all-to-all-start.4 = ((bf16[16,1,48,256]{3,2,1,0:T(8,128)(2,1)}), bf16[16,1,48,256]{3,2,1,0:T(8,128)(2,1)S(1)}, u32[]{:S(2)}, u32[]{:S(2)}) async-start(bf16[16,1,48,256]{3,2,1,0:T(8,128)(2,1)} %bitcast.89), calls=%async_computation.5 | async-start | bytes 786432 | tf_op jit(solution)/shard_map/all_to_all | solution.py:106
  596.0 20.1 %all-to-all-done.4 = bf16[16,1,48,256]{3,2,1,0:T(8,128)(2,1)S(1)} async-done(((bf16[16,1,48,256]{3,2,1,0:T(8,128)(2,1)}), bf16[16,1,48,256]{3,2,1,0:T(8,128)(2,1)S(1)}, u32[]{:S(2)}, u32[]{:S(2)}) %all-to-all-start.4) | async-done | bytes 393248 | tf_op jit(solution)/shard_map/all_to_all | solution.py:106
  616.1 1.9 gather_fusion.4
  619.8 16.1 %psum.15 = f32[256]{0:T(256)S(1)} all-reduce(f32[256]{0:T(256)S(1)} %multiply_reduce_fusion.1), channel_id=1, replica_groups=mesh['ep'=16,'mx'=4,'my'=8] {'my'}, use_global_device_ids=true, to_apply=%region_10.11 | all-reduce | flops 256 | bytes 2048 | tf_op jit(solution)/shard_map/psum | solution.py:16
  635.9 0.8 multiply_convert_fusion
  (50 shorter events, 5.7 us)
Async XLA Ops:
  7.2 6.2 copy-start
  7.2 22.9 %copy-start.5 = (f32[256]{0:T(256)S(1)}, f32[256]{0:T(256)}, u32[]{:S(2)}) copy-start(f32[256]{0:T(256)} %param.17) | copy-start | bytes 3076
  13.4 35.4 %copy-start.7 = (s32[16]{0:T(128)S(1)}, s32[16]{0:T(128)}, u32[]{:S(2)}) copy-start(s32[16]{0:T(128)} %constant.78) | copy-start | bytes 196
  13.4 35.4 %copy-start.1 = (bf16[8,44,512]{2,0,1:T(8,128)(2,1)S(1)}, bf16[8,44,512]{2,0,1:T(8,128)(2,1)}, u32[]{:S(2)}) copy-start(bf16[8,44,512]{2,0,1:T(8,128)(2,1)} %param.18) | copy-start | bytes 1081348
  33.5 36.3 %all-to-all-start = ((bf16[16,1,48,256]{3,2,1,0:T(8,128)(2,1)}), bf16[16,1,48,256]{3,2,1,0:T(8,128)(2,1)}, u32[]{:S(2)}, u32[]{:S(2)}) async-start(bf16[16,1,48,256]{3,2,1,0:T(8,128)(2,1)} %bitcast.5), calls=%async_computation | async-start | bytes 786432 | tf_op jit(solution)/shard_map/all_to_all | solution.py:57
  71.9 10.3 %copy-start.2 = (bf16[8,44,512]{2,0,1:T(8,128)(2,1)S(1)}, bf16[8,44,512]{2,0,1:T(8,128)(2,1)}, u32[]{:S(2)}) copy-start(bf16[8,44,512]{2,0,1:T(8,128)(2,1)} %param.20) | copy-start | bytes 1081348
  71.9 154.2 %all-to-all-start.1 = ((bf16[64,1,44,512]{3,2,1,0:T(8,128)(2,1)}), bf16[64,1,44,512]{3,2,1,0:T(8,128)(2,1)}, u32[]{:S(2)}, u32[]{:S(2)}) async-start(bf16[64,1,44,512]{3,2,1,0:T(8,128)(2,1)} %bitcast.87), calls=%async_computation.1 | async-start | bytes 6291456 | tf_op jit(solution)/shard_map/all_to_all | solution.py:73
  228.2 6.3 copy-start.3
  228.2 150.0 %all-to-all-start.3 = ((bf16[64,1,44,512]{3,2,1,0:T(8,128)(2,1)}), bf16[64,1,44,512]{3,2,1,0:T(8,128)(2,1)}, u32[]{:S(2)}, u32[]{:S(2)}) async-start(bf16[64,1,44,512]{3,2,1,0:T(8,128)(2,1)} %bitcast.86), calls=%async_computation.3 | async-start | bytes 6291456 | tf_op jit(solution)/shard_map/all_to_all | solution.py:79
  380.4 149.0 %all-to-all-start.2 = ((bf16[64,1,44,512]{3,2,1,0:T(8,128)(2,1)}), bf16[64,1,44,512]{3,2,1,0:T(8,128)(2,1)}, u32[]{:S(2)}, u32[]{:S(2)}) async-start(bf16[64,1,44,512]{3,2,1,0:T(8,128)(2,1)} %bitcast.85), calls=%async_computation.2 | async-start | bytes 6291456 | tf_op jit(solution)/shard_map/all_to_all | solution.py:76
  386.5 44.3 %all-gather.2.cloned.1.call-start = ((), (), s32[]{:S(2)}) async-start(), calls=%async_computation.6 | async-start | bytes 3538944 | tf_op jit(solution)/shard_map/all_gather | solution.py:58
  387.3 196.1 %reduce-scatter.2.cloned.1.call-start = ((), (), s32[]{:S(2)}) async-start(), calls=%async_computation.7 | async-start | bytes 3538944 | tf_op jit(solution)/shard_map/reduce_scatter | solution.py:101
  545.5 50.3 %copy-start.4 = (f32[256,2]{0,1:T(2,128)S(1)}, f32[256,2]{0,1:T(2,128)}, u32[]{:S(2)}) copy-start(f32[256,2]{0,1:T(2,128)} %param.22) | copy-start | bytes 6148
  545.6 90.4 %copy-start.6 = (f32[256]{0:T(256)S(1)}, f32[256]{0:T(256)}, u32[]{:S(2)}) copy-start(f32[256]{0:T(256)} %param.23) | copy-start | bytes 3076
  583.4 32.7 %all-to-all-start.4 = ((bf16[16,1,48,256]{3,2,1,0:T(8,128)(2,1)}), bf16[16,1,48,256]{3,2,1,0:T(8,128)(2,1)S(1)}, u32[]{:S(2)}, u32[]{:S(2)}) async-start(bf16[16,1,48,256]{3,2,1,0:T(8,128)(2,1)} %bitcast.89), calls=%async_computation.5 | async-start | bytes 786432 | tf_op jit(solution)/shard_map/all_to_all | solution.py:106
Sparse Core Ops, SparseCore 0:
  389.5 41.2 all-gather.1
  545.7 37.6 reduce-scatter.1
where the time goes:
time: 644 us
  waiting for transfers between devices  475 us (74%)
  starting transfers between devices  50.4 us (8%)
  local copies, waits for them, and re-layouts  43.7 us (7%)
  blocking collectives  31 us (5%)
  matrix products  24.8 us (4%)
  between operations  14.3 us (2%)
    all_to_all x1, waiting for transfers between devices, shards(): lax.all_to_all(widen_pieces(gate_weight), ('ep', 'mx'), split_axis=0, con...  141 us
    all_to_all x1, waiting for transfers between devices, shards(): lax.all_to_all(widen_pieces(down_weight), ('ep', 'mx'), split_axis=0, con...  141 us
    all_to_all x1, waiting for transfers between devices, shards(): lax.all_to_all(widen_pieces(up_weight), ('ep', 'mx'), split_axis=0, conca...  73.2 us
    all_gather x1, waiting for transfers between devices, shards(): gathered = lax.all_gather(landed, 'my', axis=3, tiled=True)  43.5 us
    reduce_scatter x1, waiting for transfers between devices, shards(): lax.psum_scatter(expert_out.astype(jnp.bfloat16), 'my', scatter_dimension...  37.8 us
    psum x2, blocking collectives, row_scale(): row_total = lax.psum(partial_sq, 'my')  31 us
    all_to_all x1, waiting for transfers between devices, shards(): lax.all_to_all(sent_back, 'ep', split_axis=0, concat_axis=0, tiled=True)  20.1 us
    all_to_all x1, waiting for transfers between devices, shards(): lax.all_to_all(packed, 'ep', split_axis=0, concat_axis=0, tiled=True)  18 us
  transfers between devices with their start and end apart: 7, of which 7 were waited for; matrix products, arithmetic and copies ran while one was open for 5% of the time, Pallas kernels for 0%

commit v1 on v0

--- a/solution.py
+++ b/solution.py
@@ -55,7 +55,9 @@
     padded = jnp.concatenate([normed, jnp.zeros((1, feat_block), jnp.bfloat16)], axis=0)
     packed = padded[source].reshape(ep_count, slot_dev, capacity, feat_block)
     landed = lax.all_to_all(packed, "ep", split_axis=0, concat_axis=0, tiled=True)
-    gathered = lax.all_gather(landed, "my", axis=3, tiled=True)
+    gathered = jnp.concatenate(
+        lax.all_to_all(jnp.stack([landed] * lax.axis_size("my")), "my", 0, 0), axis=3
+    )
     tokens_in = jnp.transpose(gathered, (1, 0, 2, 3)).reshape(slot_dev, slot_rows, D)
     split_rows = tokens_in.reshape(slot_dev, slot_rows, mx_count, width_block)
     expert_table = (

time: 644 us -> 687 us (1.067)
  the two profiles are of different devices: /device:TPU:4 before, /device:TPU:2 now
where the time goes in v1:
time: 687 us; the launch traced here: 686 us
  waiting for transfers between devices  486 us (71%)
  blocking collectives  66.9 us (10%)
  local copies, waits for them, and re-layouts  50.1 us (7%)
  starting transfers between devices  39.4 us (6%)
  matrix products  24.8 us (4%)
  between operations  14.3 us (2%)
    all_to_all x1, waiting for transfers between devices, shards(): lax.all_to_all(widen_pieces(gate_weight), ('ep', 'mx'), split_axis=0, con...  142 us
    all_to_all x1, waiting for transfers between devices, shards(): lax.all_to_all(widen_pieces(down_weight), ('ep', 'mx'), split_axis=0, con...  141 us
    all_to_all x1, waiting for transfers between devices, shards(): lax.all_to_all(widen_pieces(up_weight), ('ep', 'mx'), split_axis=0, conca...  114 us
    all_to_all x1, blocking collectives, shards(): lax.all_to_all(packed, 'ep', split_axis=0, concat_axis=0, tiled=True)  36 us
    all_to_all x1, waiting for transfers between devices, shards(): lax.all_to_all(jnp.stack([landed] * lax.axis_size('my')), 'my', 0, 0)  35.5 us
    reduce_scatter x1, waiting for transfers between devices, shards(): lax.psum_scatter(expert_out.astype(jnp.bfloat16), 'my', scatter_dimension...  33.3 us
    psum x2, blocking collectives, row_scale(): row_total = lax.psum(partial_sq, 'my')  30.9 us
    all_to_all x1, waiting for transfers between devices, shards(): lax.all_to_all(sent_back, 'ep', split_axis=0, concat_axis=0, tiled=True)  20.1 us
  transfers between devices with their start and end apart: 6, of which 6 were waited for; matrix products, arithmetic and copies ran while one was open for 6% of the time, Pallas kernels for 0%

profile of v1, /device:TPU:2, one launch (start us, length us, event | category | flops | bytes accessed | tf_op | source)
XLA Modules:
  0.0 685.6 jit_solution(5144222191437310215)
XLA Ops:
  9.1 1.1 reduce-window.6
  10.9 2.4 scatter_custom_fusion
  13.4 1.7 multiply_reduce_fusion.2
  15.1 14.9 %psum.14 = f32[256]{0:T(256)S(1)} all-reduce(f32[256]{0:T(256)S(1)} %get-tuple-element.4), channel_id=1, replica_groups=mesh['ep'=16,'mx'=4,'my'=8] {'my'}, use_global_device_ids=true, to_apply=%region_2.0 | all-reduce | flops 256 | bytes 2048 | tf_op jit(solution)/shard_map/psum | solution.py:16
  30.1 2.7 gather_fusion
  32.8 36.0 %all_to_all.33 = bf16[16,1,48,256]{3,2,1,0:T(8,128)(2,1)S(1)} all-to-all(bf16[16,1,48,256]{3,2,1,0:T(8,128)(2,1)S(1)} %bitcast.94), channel_id=1, replica_groups=mesh['ep'=16,'mx'=4,'my'=8] {'ep'}, dimensions={0} | all-to-all | bytes 786432 | tf_op jit(solution)/shard_map/all_to_all | solution.py:57
  68.8 1.9 stack.2
  70.7 5.7 all-to-all-start.1
  76.5 2.6 gather_fusion.1
  79.5 35.5 %all-to-all-done.1 = bf16[8,16,1,48,256]{4,3,1,2,0:T(8,128)(2,1)} async-done(((bf16[8,16,1,48,256]{4,3,1,2,0:T(8,128)(2,1)}), bf16[8,16,1,48,256]{4,3,1,2,0:T(8,128)(2,1)}, u32[]{:S(2)}, u32[]{:S(2)}) %all-to-all-start.1) | async-done | bytes 3145760 | tf_op jit(solution)/shard_map/all_to_all | solution.py:59
  115.0 2.1 broadcast_in_dim.59
  117.1 9.0 %all-to-all-start.2 = ((bf16[64,1,44,512]{3,2,1,0:T(8,128)(2,1)}), bf16[64,1,44,512]{3,2,1,0:T(8,128)(2,1)}, u32[]{:S(2)}, u32[]{:S(2)}) async-start(bf16[64,1,44,512]{3,2,1,0:T(8,128)(2,1)} %bitcast.91), calls=%async_computation.2 | async-start | bytes 6291456 | tf_op jit(solution)/shard_map/all_to_all | solution.py:75
  126.1 2.6 gather_fusion.3
  129.2 141.8 %all-to-all-done.2 = bf16[64,1,44,512]{3,2,1,0:T(8,128)(2,1)} async-done(((bf16[64,1,44,512]{3,2,1,0:T(8,128)(2,1)}), bf16[64,1,44,512]{3,2,1,0:T(8,128)(2,1)}, u32[]{:S(2)}, u32[]{:S(2)}) %all-to-all-start.2) | async-done | bytes 2883616 | tf_op jit(solution)/shard_map/all_to_all | solution.py:75
  270.9 2.1 broadcast_in_dim.67
  273.0 6.3 all-to-all-start.4
  279.3 2.6 gather_fusion.2
  282.3 141.3 %all-to-all-done.4 = bf16[64,1,44,512]{3,2,1,0:T(8,128)(2,1)} async-done(((bf16[64,1,44,512]{3,2,1,0:T(8,128)(2,1)}), bf16[64,1,44,512]{3,2,1,0:T(8,128)(2,1)}, u32[]{:S(2)}, u32[]{:S(2)}) %all-to-all-start.4) | async-done | bytes 2883616 | tf_op jit(solution)/shard_map/all_to_all | solution.py:81
  423.7 2.1 broadcast_in_dim.63
  425.8 6.1 all-to-all-start.3
  431.9 5.3 copy.33
  437.3 6.0 reshape.203
  443.2 5.7 copy.62
  448.9 6.7 dot_general.20
  455.6 6.9 %fusion.2 = f32[768,16,44,1]{0,2,3,1:T(8,128)} fusion(bf16[768,4,512]{2,1,0:T(4,128)(2,1)} %reshape.203, bf16[16,4,44,512]{3,2,1,0:T(8,128)(2,1)} %bitcast.84), kind=kOutput, calls=%fused_computation.9 | convolution fusion | flops 2214592512 | bytes 8192000 | tf_op jit(solution)/shard_map/jrad,sajfd->jrsf/dot_general | solution.py:86
  462.5 113.7 %all-to-all-done.3 = bf16[64,1,44,512]{3,2,1,0:T(8,128)(2,1)} async-done(((bf16[64,1,44,512]{3,2,1,0:T(8,128)(2,1)}), bf16[64,1,44,512]{3,2,1,0:T(8,128)(2,1)}, u32[]{:S(2)}, u32[]{:S(2)}) %all-to-all-start.3) | async-done | bytes 2883616 | tf_op jit(solution)/shard_map/all_to_all | solution.py:78
  576.2 16.1 %fusion.7 = bf16[1,768,2048]{2,1,0:T(8,128)(2,1)} fusion(bf16[2048,44,16]{0,2,1:T(8,128)(2,1)} %dot_general.20, f32[768,16,44,1]{0,2,3,1:T(8,128)} %fusion.2, bf16[768,4,512]{2,1,0:T(4,128)(2,1)} %reshape.203, bf16[16,4,44,512]{3,2,1,0:T(8,128)(2,1)} %bitcast.87), kind=kOutput, calls=%fused_computation.14 | convolution fusion | flops 4434001920 | bytes 14221312 | tf_op jit(solution)/shard_map/jrsf,sajfd->jrad/dot_general | solution.py:99
  592.3 33.3 %reduce-scatter.2.cloned.1.call-done = bf16[1,768,256]{2,1,0:T(8,128)(2,1)} async-done(((bf16[1,768,2048]{2,1,0:T(8,128)(2,1)}), bf16[1,768,256]{2,1,0:T(8,128)(2,1)}) %reduce-scatter.2.cloned.1.call-update) | async-done | bytes 393232 | tf_op jit(solution)/shard_map/reduce_scatter | solution.py:103
  625.6 12.3 %all-to-all-start.5 = ((bf16[16,1,48,256]{3,2,1,0:T(8,128)(2,1)}), bf16[16,1,48,256]{3,2,1,0:T(8,128)(2,1)S(1)}, u32[]{:S(2)}, u32[]{:S(2)}) async-start(bf16[16,1,48,256]{3,2,1,0:T(8,128)(2,1)} %bitcast.95), calls=%async_computation.6 | async-start | bytes 786432 | tf_op jit(solution)/shard_map/all_to_all | solution.py:108
  638.1 20.1 %all-to-all-done.5 = bf16[16,1,48,256]{3,2,1,0:T(8,128)(2,1)S(1)} async-done(((bf16[16,1,48,256]{3,2,1,0:T(8,128)(2,1)}), bf16[16,1,48,256]{3,2,1,0:T(8,128)(2,1)S(1)}, u32[]{:S(2)}, u32[]{:S(2)}) %all-to-all-start.5) | async-done | bytes 393248 | tf_op jit(solution)/shard_map/all_to_all | solution.py:108
  658.3 1.9 gather_fusion.4
  662.0 16.0 %psum.15 = f32[256]{0:T(256)S(1)} all-reduce(f32[256]{0:T(256)S(1)} %multiply_reduce_fusion.1), channel_id=1, replica_groups=mesh['ep'=16,'mx'=4,'my'=8] {'my'}, use_global_device_ids=true, to_apply=%region_10.11 | all-reduce | flops 256 | bytes 2048 | tf_op jit(solution)/shard_map/psum | solution.py:16
  (50 shorter events, 6.7 us)
Async XLA Ops:
  7.2 6.2 copy-start
  7.2 22.8 %copy-start.5 = (f32[256]{0:T(256)S(1)}, f32[256]{0:T(256)}, u32[]{:S(2)}) copy-start(f32[256]{0:T(256)} %param.17) | copy-start | bytes 3076
  70.7 5.8 copy-start.7
  70.7 5.8 copy-start.1
  70.7 44.3 %all-to-all-start.1 = ((bf16[8,16,1,48,256]{4,3,1,2,0:T(8,128)(2,1)}), bf16[8,16,1,48,256]{4,3,1,2,0:T(8,128)(2,1)}, u32[]{:S(2)}, u32[]{:S(2)}) async-start(bf16[8,16,1,48,256]{4,3,1,2,0:T(8,128)(2,1)} %stack.2), calls=%async_computation.1 | async-start | bytes 6291456 | tf_op jit(solution)/shard_map/all_to_all | solution.py:59
  117.1 9.0 %copy-start.2 = (bf16[8,44,512]{2,0,1:T(8,128)(2,1)S(1)}, bf16[8,44,512]{2,0,1:T(8,128)(2,1)}, u32[]{:S(2)}) copy-start(bf16[8,44,512]{2,0,1:T(8,128)(2,1)} %param.20) | copy-start | bytes 1081348
  117.1 153.8 %all-to-all-start.2 = ((bf16[64,1,44,512]{3,2,1,0:T(8,128)(2,1)}), bf16[64,1,44,512]{3,2,1,0:T(8,128)(2,1)}, u32[]{:S(2)}, u32[]{:S(2)}) async-start(bf16[64,1,44,512]{3,2,1,0:T(8,128)(2,1)} %bitcast.91), calls=%async_computation.2 | async-start | bytes 6291456 | tf_op jit(solution)/shard_map/all_to_all | solution.py:75
  273.0 6.3 copy-start.3
  273.0 150.6 %all-to-all-start.4 = ((bf16[64,1,44,512]{3,2,1,0:T(8,128)(2,1)}), bf16[64,1,44,512]{3,2,1,0:T(8,128)(2,1)}, u32[]{:S(2)}, u32[]{:S(2)}) async-start(bf16[64,1,44,512]{3,2,1,0:T(8,128)(2,1)} %bitcast.90), calls=%async_computation.4 | async-start | bytes 6291456 | tf_op jit(solution)/shard_map/all_to_all | solution.py:81
  425.8 150.4 %all-to-all-start.3 = ((bf16[64,1,44,512]{3,2,1,0:T(8,128)(2,1)}), bf16[64,1,44,512]{3,2,1,0:T(8,128)(2,1)}, u32[]{:S(2)}, u32[]{:S(2)}) async-start(bf16[64,1,44,512]{3,2,1,0:T(8,128)(2,1)} %bitcast.89), calls=%async_computation.3 | async-start | bytes 6291456 | tf_op jit(solution)/shard_map/all_to_all | solution.py:78
  431.9 193.8 %reduce-scatter.2.cloned.1.call-start = ((), (), s32[]{:S(2)}) async-start(), calls=%async_computation.7 | async-start | bytes 3538944 | tf_op jit(solution)/shard_map/reduce_scatter | solution.py:103
  592.3 45.6 %copy-start.4 = (f32[256,2]{0,1:T(2,128)S(1)}, f32[256,2]{0,1:T(2,128)}, u32[]{:S(2)}) copy-start(f32[256,2]{0,1:T(2,128)} %param.22) | copy-start | bytes 6148
  592.3 85.7 %copy-start.6 = (f32[256]{0:T(256)S(1)}, f32[256]{0:T(256)}, u32[]{:S(2)}) copy-start(f32[256]{0:T(256)} %param.23) | copy-start | bytes 3076
  625.6 32.6 %all-to-all-start.5 = ((bf16[16,1,48,256]{3,2,1,0:T(8,128)(2,1)}), bf16[16,1,48,256]{3,2,1,0:T(8,128)(2,1)S(1)}, u32[]{:S(2)}, u32[]{:S(2)}) async-start(bf16[16,1,48,256]{3,2,1,0:T(8,128)(2,1)} %bitcast.95), calls=%async_computation.6 | async-start | bytes 786432 | tf_op jit(solution)/shard_map/all_to_all | solution.py:108
Sparse Core Ops, SparseCore 0:
  592.4 33.1 reduce-scatter.1
